TPU v7x, 32 devices: a whole 2x2x4 slice. The times are simulated.
32 devices in a mesh: batch: 4 (over x, core), centers: 8 (over z, y).
Axes of the slice: x: 2, y: 2, z: 4, core: 2. Of those that a mesh axis runs over, the one named last changes fastest.
Arguments:
- pool_features: float32 [32768, 128], P(('batch', 'centers')), may hold values from -14 to 14
- pool_targets: float32 [32768, 64], P(('batch', 'centers')), may hold values from -6 to 6
- batch_index: int32 [2048], P(('batch', 'centers')), may hold values from 0 to 1023
- centers: float32 [4096, 128], P('centers'), may hold values from -14 to 14
- weights: float32 [4096, 64], P('centers'), as said below
- eig_vectors: float32 [4096, 1024], P(('batch', 'centers')), may hold values from -0.09375 to 0.09375
- eig_scale: float32 [1024], replicated, may hold values from 0.5 to 4
- nys_owner: int32 [4096, 1], P(('batch', 'centers')), may hold values from 0 to 7; in each aligned block of 128 rows (0 to 127, 128 to 255, ...) at most 32 rows name the same one
- nys_offset: int32 [4096], P(('batch', 'centers')), may hold values from 0 to 511
Outputs:
- residual_out: float32 [2048, 64], P(('batch', 'centers'))
- update: float32 [4096, 64], P('centers')
Inputs may be any that keep to these rules, and one draw needn't show every extreme that they name: `nys_owner`: among the 128 rows of one device no owner is named more than 32 times; on some devices one owner is named exactly 32 times. `weights`: every column sums to zero.
All inputs are finite; a program needn't handle non-finite values.
Results may differ from a plain program's by a relative error of at most 0.0003.
Values sent between devices are 32-bit elements; how exact they have to be, the bound alone decides.
A program may use at most 64 MiB of HBM per device.

v0:
```python
import math
import jax
import jax.numpy as jnp
from jax import lax
from jax.sharding import PartitionSpec as P

DEPTH = 3
epsilon = 1e-06
highest = lax.Precision.HIGHEST


def kernel_rows(row_block, center_block, center_norm):
    inner_prod = (
        lax.dot_general(
            row_block,
            center_block,
            (((1,), (1,)), ((), ())),
            precision=highest,
            preferred_element_type=jnp.float32,
        )
        / row_block.shape[1]
    )
    row_norm = jnp.mean(row_block * row_block, axis=1) + epsilon
    norm_scale = jnp.sqrt(row_norm[:, None] * center_norm[None, :])
    sigma_now = inner_prod
    tangent = inner_prod
    for depth_step in range(DEPTH):
        cosine = sigma_now / norm_scale
        arc_angle = jnp.arccos(cosine)
        remain = (math.pi - arc_angle) / math.pi
        sigma_now = (
            norm_scale
            * (jnp.sqrt(1.0 - cosine * cosine) + (math.pi - arc_angle) * cosine)
            / math.pi
        )
        tangent = sigma_now + tangent * remain
    return tangent


def per_device(
    pool_features,
    pool_targets,
    batch_index,
    centers,
    weights,
    eig_vectors,
    eig_scale,
    nys_owner,
    nys_offset,
):
    local_rows = pool_features[batch_index]
    local_targets = pool_targets[batch_index]
    row_count = local_rows.shape[0]
    group_size = lax.axis_size("centers")
    rows_total = row_count * group_size * lax.axis_size("batch")
    center_count = centers.shape[0]
    outputs = weights.shape[1]
    center_norm = jnp.mean(centers * centers, axis=1) + epsilon
    kernel = kernel_rows(
        lax.all_gather(local_rows, "centers", axis=0, tiled=True), centers, center_norm
    )
    partial_pred = jnp.dot(kernel, weights, precision=highest, preferred_element_type=jnp.float32)
    all_targets = lax.all_gather(local_targets, "centers", axis=0, tiled=True)
    prediction = lax.psum(partial_pred, "centers")
    residual = prediction - all_targets
    own_residual = lax.dynamic_slice_in_dim(
        residual, lax.axis_index("centers") * row_count, row_count, 0
    )
    grads_part = lax.dot_general(
        kernel,
        residual,
        (((0,), (0,)), ((), ())),
        precision=highest,
        preferred_element_type=jnp.float32,
    ) / math.sqrt(rows_total)
    grads = lax.psum(grads_part, "batch")
    owner = nys_owner[:, 0]
    slots = max(2, 2 * owner.shape[0] // group_size)
    owner_hot = (owner[:, None] == jnp.arange(group_size, dtype=jnp.int32)[None, :]).astype(
        jnp.int32
    )
    slot_rank = jnp.sum((jnp.cumsum(owner_hot, axis=0) - owner_hot) * owner_hot, axis=1)
    requests = jnp.zeros((group_size, slots), jnp.int32).at[owner, slot_rank].set(nys_offset)
    received = lax.all_to_all(requests, "centers", split_axis=0, concat_axis=0, tiled=True)
    found = grads[received]
    returned = lax.all_to_all(found, "centers", split_axis=0, concat_axis=0, tiled=True)
    picked_grads = returned[owner, slot_rank]
    coeff_part = lax.dot_general(
        eig_vectors,
        picked_grads,
        (((0,), (0,)), ((), ())),
        precision=highest,
        preferred_element_type=jnp.float32,
    )
    coeff = lax.psum(coeff_part, ("batch", "centers"))
    corr_rows = jnp.dot(
        eig_vectors,
        eig_scale[:, None] * coeff,
        precision=highest,
        preferred_element_type=jnp.float32,
    )
    outgoing = (
        jnp.zeros((group_size, slots, outputs), jnp.float32).at[owner, slot_rank].set(corr_rows)
    )
    incoming = lax.all_to_all(outgoing, "centers", split_axis=0, concat_axis=0, tiled=True)
    corr_part = jnp.zeros((center_count, outputs), jnp.float32).at[received].add(incoming)
    correction = lax.psum(corr_part, "batch")
    return (own_residual, correction - grads)


def solution(mesh):
    placed = (
        P(("batch", "centers"), None),
        P(("batch", "centers"), None),
        P(("batch", "centers")),
        P("centers", None),
        P("centers", None),
        P(("batch", "centers"), None),
        P(),
        P(("batch", "centers"), None),
        P(("batch", "centers")),
    )
    return jax.shard_map(
        per_device,
        mesh=mesh,
        in_specs=placed,
        out_specs=(P(("batch", "centers"), None), P("centers", None)),
        check_vma=False,
    )
```

profile of v0, /device:TPU:0, one launch (start us, length us, event | category | flops | bytes accessed | tf_op | source)
XLA Modules:
  0.0 387.0 jit_solution(5106888059048131326)
XLA Ops:
  7.2 0.7 copy-done.6
  7.9 0.1 fusion.4
  8.0 0.2 reduce_window_sum.11
  8.2 0.2 select_reduce_fusion
  8.4 0.6 broadcast.104
  9.0 0.1 copy-done.8
  9.0 19.9 %scatter_fusion = s32[8,32]{1,0:T(8,128)} fusion(s32[8,32]{1,0:T(8,128)} %broadcast.104, s32[128]{0:T(128)S(1)} %get-tuple-element.8, s32[128]{0:T(128)S(1)} %copy-done.8), kind=kCustom, calls=%fused_computation.4 | custom fusion | bytes 2560 | tf_op jit(solution)/shard_map/scatter | solution.py:83
  28.9 7.4 %all-to-all-start = ((s32[8,1,32]{2,1,0:T(1,128)}), s32[8,1,32]{2,1,0:T(1,128)S(1)}, u32[]{:S(2)}, u32[]{:S(2)}) async-start(s32[8,1,32]{2,1,0:T(1,128)} %bitcast.4), calls=%async_computation | async-start | bytes 8192 | tf_op jit(solution)/shard_map/all_to_all | solution.py:84
  36.4 0.1 multiply_reduce_fusion
  36.6 0.6 gather_fusion
  37.2 31.2 %all-gather = f32[512,128]{1,0:T(8,128)S(1)} all-gather(f32[64,128]{1,0:T(8,128)S(1)} %gather_fusion), channel_id=2, replica_groups=mesh['batch'=4,'centers'=8] {'centers'}, dimensions={0}, use_global_device_ids=true | all-gather | bytes 294912 | tf_op jit(solution)/shard_map/all_gather | solution.py:60
  68.4 0.1 multiply_reduce_fusion.1
  68.6 8.9 %multiply_add_fusion = f32[512,512]{1,0:T(8,128)S(1)} fusion(f32[512,128]{1,0:T(8,128)S(1)} %all-gather, f32[512,128]{1,0:T(8,128)S(1)} %copy-done.3, f32[512]{0:T(512)S(1)} %multiply_add_fusion.1, f32[512]{0:T(512)S(1)} %multiply_add_fusion.2), kind=kOutput, calls=%fused_computation.11 | convolution fusion | flops 414187520 | bytes 1576960 | tf_op jit(solution)/shard_map/dot_general | solution.py:14
  77.5 1.8 fusion.8
  79.4 0.2 copy.23
  79.6 0.6 gather_fusion.1
  80.2 30.8 %all-gather.1 = f32[512,64]{1,0:T(8,128)S(1)} all-gather(f32[64,64]{1,0:T(8,128)S(1)} %gather_fusion.1), channel_id=3, replica_groups=mesh['batch'=4,'centers'=8] {'centers'}, dimensions={0}, use_global_device_ids=true | all-gather | bytes 147456 | tf_op jit(solution)/shard_map/all_gather | solution.py:63
  111.1 0.1 copy.24
  111.2 0.1 reshape.100
  111.3 39.5 %all-reduce.5.cloned.1.call-done = f32[512,64]{0,1:T(8,128)} async-done(((f32[512,64]{0,1:T(8,128)}), f32[512,64]{0,1:T(8,128)}) %all-reduce.5.cloned.1.call-update) | async-done | bytes 131088 | tf_op jit(solution)/shard_map/psum | solution.py:64
  150.8 0.9 sub.36
  151.7 1.5 convolution_multiply_fusion.1
  153.2 0.0 all-reduce.9.cloned.1.call-start
  153.3 31.3 %all-reduce.7.cloned.1.call-done = f32[512,64]{0,1:T(8,128)} async-done(((f32[512,64]{0,1:T(8,128)}), f32[512,64]{0,1:T(8,128)}) %all-reduce.7.cloned.1.call-update) | async-done | bytes 131088 | tf_op jit(solution)/shard_map/psum | solution.py:76
  184.6 1.0 copy.26
  185.6 0.7 gather_fusion.2
  186.3 0.1 reshape.114
  186.5 12.2 %all_to_all.22 = f32[8,1,2048]{2,1,0:T(1,128)S(1)} all-to-all(f32[8,1,2048]{2,1,0:T(1,128)S(1)} %reshape.114), channel_id=1, replica_groups=mesh['batch'=4,'centers'=8] {'centers'}, dimensions={0} | all-to-all | bytes 131072 | tf_op jit(solution)/shard_map/all_to_all | solution.py:86
  198.7 0.5 broadcast.212
  199.2 0.8 reduce
  200.0 0.1 reshape.115
  200.1 1.2 gather_fusion.3
  201.3 1.1 convolution_bitcast_fusion
  202.5 123.4 %all-reduce.9.cloned.1.call-done = f32[1024,64]{0,1:T(8,128)} async-done(((f32[1024,64]{0,1:T(8,128)}), f32[1024,64]{0,1:T(8,128)}) %all-reduce.9.cloned.1.call-update) | async-done | bytes 262160 | tf_op jit(solution)/shard_map/psum | solution.py:95
  325.9 1.6 convolution_bitcast_fusion.1
  327.5 0.1 copy.27
  327.7 6.9 %scatter_fusion.1 = f32[8,32,64]{2,1,0:T(8,128)S(1)} fusion(f32[8,32,64]{2,1,0:T(8,128)S(1)} %broadcast_in_dim.8, s32[128]{0:T(128)S(1)} %get-tuple-element.8, f32[128,64]{1,0:T(8,128)S(1)} %copy.27), kind=kCustom, calls=%fused_computation.5 | custom fusion | bytes 99328 | tf_op jit(solution)/shard_map/scatter | solution.py:103
  334.6 0.8 reshape.116
  335.3 4.5 %all-to-all-start.2 = ((f32[8,1,2048]{2,1,0:T(1,128)}), f32[8,1,2048]{2,1,0:T(1,128)S(1)}, u32[]{:S(2)}, u32[]{:S(2)}) async-start(f32[8,1,2048]{2,1,0:T(1,128)} %reshape.116), calls=%async_computation.2 | async-start | bytes 131072 | tf_op jit(solution)/shard_map/all_to_all | solution.py:105
  339.9 6.9 %all-to-all-done.2 = f32[8,1,2048]{2,1,0:T(1,128)S(1)} async-done(((f32[8,1,2048]{2,1,0:T(1,128)}), f32[8,1,2048]{2,1,0:T(1,128)S(1)}, u32[]{:S(2)}, u32[]{:S(2)}) %all-to-all-start.2) | async-done | bytes 65568 | tf_op jit(solution)/shard_map/all_to_all | solution.py:105
  346.7 0.8 reduce.1
  347.6 0.1 reshape.117
  347.6 1.7 scatter_custom_fusion.2
  349.4 0.8 copy.28
  350.2 0.1 constant_dynamic-slice_fusion
  350.3 0.7 copy.29
  351.0 27.9 %all-reduce.11.cloned.1.call-done = f32[512,64]{0,1:T(8,128)} async-done(((f32[512,64]{0,1:T(8,128)}), f32[512,64]{0,1:T(8,128)}) %all-reduce.11.cloned.1.call-update) | async-done | bytes 131088 | tf_op jit(solution)/shard_map/psum | solution.py:107
  378.9 1.6 sub.38
  (34 shorter events, 0.3 us)
Async XLA Ops:
  7.2 194.2 %copy-start = (f32[128,1024]{1,0:T(8,128)S(1)}, f32[128,1024]{1,0:T(8,128)}, u32[]{:S(2)}) copy-start(f32[128,1024]{1,0:T(8,128)} %param.14) | copy-start | bytes 1572868
  7.2 0.7 copy-start.6
  8.3 0.7 copy-start.8
  9.0 27.4 %copy-start.3 = (f32[512,128]{1,0:T(8,128)S(1)}, f32[512,128]{1,0:T(8,128)}, u32[]{:S(2)}) copy-start(f32[512,128]{1,0:T(8,128)} %param.12) | copy-start | bytes 786436
  9.0 27.6 %copy-start.5 = (f32[1024,128]{1,0:T(8,128)S(1)}, f32[1024,128]{1,0:T(8,128)}, u32[]{:S(2)}) copy-start(f32[1024,128]{1,0:T(8,128)} %param.9) | copy-start | bytes 1572868
  28.9 7.5 %copy-start.9 = (s32[64]{0:T(128)S(1)}, s32[64]{0:T(128)}, u32[]{:S(2)}) copy-start(s32[64]{0:T(128)} %param.11) | copy-start | bytes 772
  28.9 82.3 %all-to-all-start = ((s32[8,1,32]{2,1,0:T(1,128)}), s32[8,1,32]{2,1,0:T(1,128)S(1)}, u32[]{:S(2)}, u32[]{:S(2)}) async-start(s32[8,1,32]{2,1,0:T(1,128)} %bitcast.4), calls=%async_computation | async-start | bytes 8192 | tf_op jit(solution)/shard_map/all_to_all | solution.py:84
  36.3 114.5 %all-reduce.5.cloned.1.call-start = ((), (), s32[]{:S(2)}) async-start(), calls=%async_computation.3 | async-start | bytes 262144 | tf_op jit(solution)/shard_map/psum | solution.py:64
  68.6 8.9 %copy-start.4 = (f32[512,64]{0,1:T(8,128)S(1)}, f32[512,64]{0,1:T(8,128)}, u32[]{:S(2)}) copy-start(f32[512,64]{0,1:T(8,128)} %param.13) | copy-start | bytes 393220
  77.5 1.9 copy-start.2
  79.4 105.2 %all-reduce.7.cloned.1.call-start = ((), (), s32[]{:S(2)}) async-start(), calls=%async_computation.4 | async-start | bytes 262144 | tf_op jit(solution)/shard_map/psum | solution.py:76
  153.2 172.7 %all-reduce.9.cloned.1.call-start = ((), (), s32[]{:S(2)}) async-start(), calls=%async_computation.5 | async-start | bytes 524288 | tf_op jit(solution)/shard_map/psum | solution.py:95
  202.5 123.4 %copy-start.7 = (f32[1024]{0:T(1024)S(1)}, f32[1024]{0:T(1024)}, u32[]{:S(2)}) copy-start(f32[1024]{0:T(1024)} %param.15) | copy-start | bytes 12292
  335.3 11.4 %all-to-all-start.2 = ((f32[8,1,2048]{2,1,0:T(1,128)}), f32[8,1,2048]{2,1,0:T(1,128)S(1)}, u32[]{:S(2)}, u32[]{:S(2)}) async-start(f32[8,1,2048]{2,1,0:T(1,128)} %reshape.116), calls=%async_computation.2 | async-start | bytes 131072 | tf_op jit(solution)/shard_map/all_to_all | solution.py:105
  339.8 39.0 %all-reduce.11.cloned.1.call-start = ((), (), s32[]{:S(2)}) async-start(), calls=%async_computation.6 | async-start | bytes 262144 | tf_op jit(solution)/shard_map/psum | solution.py:107
  350.1 28.7 %copy-start.1 = (f32[512,64]{0,1:T(8,128)S(1)}, f32[512,64]{0,1:T(8,128)}, u32[]{:S(2)}) copy-start(f32[512,64]{0,1:T(8,128)} %all-reduce.7.cloned.1.call-done) | copy-start | bytes 393220
Sparse Core Ops, SparseCore 0:
  79.5 71.2 all-reduce.4
  153.7 30.8 all-reduce.6
  202.6 123.2 all-reduce.8
  350.3 28.5 all-reduce.10
where the time goes:
time: 388 us; the launch traced here: 387 us
  waiting for transfers between devices  229 us (59%)
  blocking collectives  74.3 us (19%)
  local copies, waits for them, and re-layouts  36 us (9%)
  matrix products  14.9 us (4%)
  between operations  14 us (4%)
  starting transfers between devices  12.1 us (3%)
  other arithmetic  6.6 us (2%)
    psum x1, waiting for transfers between devices, per_device(): coeff = lax.psum(coeff_part, ('batch', 'centers'))  123 us
    psum x1, waiting for transfers between devices, per_device(): prediction = lax.psum(partial_pred, 'centers')  39.5 us
    psum x1, waiting for transfers between devices, per_device(): grads = lax.psum(grads_part, 'batch')  31.3 us
    all_gather x1, blocking collectives, per_device(): lax.all_gather(local_rows, 'centers', axis=0, tiled=True)  31.2 us
    all_gather x1, blocking collectives, per_device(): all_targets = lax.all_gather(local_targets, 'centers', axis=0, tiled=True)  30.8 us
    psum x1, waiting for transfers between devices, per_device(): correction = lax.psum(corr_part, 'batch')  27.9 us
    scatter x1, local copies, waits for them, and re-layouts, per_device(): jnp.zeros((group_size, slots), jnp.int32).at[owner, slot_rank]  19.9 us
    all_to_all x1, blocking collectives, per_device(): lax.all_to_all(found, 'centers', split_axis=0, concat_axis=0, tiled=True)  12.2 us
  transfers between devices with their start and end apart: 6, of which 5 were waited for; matrix products, arithmetic and copies ran while one was open for 3% of the time, Pallas kernels for 0%

commit v1 on v0

--- a/solution.py
+++ b/solution.py
@@ -104,7 +104,10 @@
     )
     incoming = lax.all_to_all(outgoing, "centers", split_axis=0, concat_axis=0, tiled=True)
     corr_part = jnp.zeros((center_count, outputs), jnp.float32).at[received].add(incoming)
-    correction = lax.psum(corr_part, "batch")
+    size, correction = (lax.axis_size("batch"), corr_part)
+    for far in [1 << k for k in range(size.bit_length() - 1)]:
+        route = [(i, i ^ far) for i in range(size)]
+        correction = correction + lax.ppermute(correction, "batch", route)
     return (own_residual, correction - grads)
 
 

time: 388 us -> 364 us (0.938)
  waiting for transfers between devices: 229 us -> 200 us
  blocking collectives: 74.3 us -> 85.5 us
    psum x1 -> x0, waiting for transfers between devices: 27.9 us -> none  [per_device(): correction = lax.psum(corr_part, 'batch')]
    all_to_all x0 -> x1, blocking collectives: none -> 11.2 us  [per_device(): lax.all_to_all(outgoing, 'centers', split_axis=0, concat_axis=0, tiled=True)]
    all_to_all x1 -> x0, waiting for transfers between devices: 6.86 us -> none  [per_device(): lax.all_to_all(outgoing, 'centers', split_axis=0, concat_axis=0, tiled=True)]
    ppermute x0 -> x2, waiting for transfers between devices: none -> 5.48 us  [per_device(): correction = correction + lax.ppermute(correction, 'batch', route)]
    all_to_all x1 -> x0, starting transfers between devices: 4.52 us -> none  [per_device(): lax.all_to_all(outgoing, 'centers', split_axis=0, concat_axis=0, tiled=True)]
  transfers between devices with their start and end apart: 6 -> 6, of which waited for: 5 -> 5; matrix products, arithmetic and copies ran while one was open for 3% -> 4% of each run, Pallas kernels for 0% -> 0%
where the time goes in v1:
time: 364 us; the launch traced here: 363 us
  waiting for transfers between devices  200 us (55%)
  blocking collectives  85.5 us (23%)
  local copies, waits for them, and re-layouts  34.7 us (10%)
  matrix products  14.9 us (4%)
  between operations  14 us (4%)
  starting transfers between devices  8.32 us (2%)
  other arithmetic  5.72 us (2%)
    psum x1, waiting for transfers between devices, per_device(): coeff = lax.psum(coeff_part, ('batch', 'centers'))  123 us
    psum x1, waiting for transfers between devices, per_device(): prediction = lax.psum(partial_pred, 'centers')  39.5 us
    psum x1, waiting for transfers between devices, per_device(): grads = lax.psum(grads_part, 'batch')  31.3 us
    all_gather x1, blocking collectives, per_device(): lax.all_gather(local_rows, 'centers', axis=0, tiled=True)  31.2 us
    all_gather x1, blocking collectives, per_device(): all_targets = lax.all_gather(local_targets, 'centers', axis=0, tiled=True)  30.8 us
    scatter x1, local copies, waits for them, and re-layouts, per_device(): jnp.zeros((group_size, slots), jnp.int32).at[owner, slot_rank]  19.9 us
    all_to_all x1, blocking collectives, per_device(): lax.all_to_all(found, 'centers', split_axis=0, concat_axis=0, tiled=True)  12.2 us
    all_to_all x1, blocking collectives, per_device(): lax.all_to_all(outgoing, 'centers', split_axis=0, concat_axis=0, tiled=True)  11.2 us
  transfers between devices with their start and end apart: 6, of which 5 were waited for; matrix products, arithmetic and copies ran while one was open for 4% of the time, Pallas kernels for 0%

profile of v1, /device:TPU:0, one launch (start us, length us, event | category | flops | bytes accessed | tf_op | source)
XLA Modules:
  0.0 362.9 jit_solution(18172965295878565667)
XLA Ops:
  7.2 0.7 copy-done.6
  7.9 0.1 fusion.4
  8.0 0.2 reduce_window_sum.11
  8.2 0.2 select_reduce_fusion
  8.4 0.6 broadcast.104
  9.0 19.9 %scatter_fusion = s32[8,32]{1,0:T(8,128)} fusion(s32[8,32]{1,0:T(8,128)} %broadcast.104, s32[128]{0:T(128)S(1)} %get-tuple-element.8, s32[128]{0:T(128)S(1)} %copy-done.8), kind=kCustom, calls=%fused_computation.4 | custom fusion | bytes 2560 | tf_op jit(solution)/shard_map/scatter | solution.py:83
  28.9 7.4 %all-to-all-start = ((s32[8,1,32]{2,1,0:T(1,128)}), s32[8,1,32]{2,1,0:T(1,128)S(1)}, u32[]{:S(2)}, u32[]{:S(2)}) async-start(s32[8,1,32]{2,1,0:T(1,128)} %bitcast.4), calls=%async_computation | async-start | bytes 8192 | tf_op jit(solution)/shard_map/all_to_all | solution.py:84
  36.4 0.1 multiply_reduce_fusion
  36.6 0.6 gather_fusion
  37.2 31.2 %all-gather = f32[512,128]{1,0:T(8,128)S(1)} all-gather(f32[64,128]{1,0:T(8,128)S(1)} %gather_fusion), channel_id=2, replica_groups=mesh['batch'=4,'centers'=8] {'centers'}, dimensions={0}, use_global_device_ids=true | all-gather | bytes 294912 | tf_op jit(solution)/shard_map/all_gather | solution.py:60
  68.4 0.1 multiply_reduce_fusion.1
  68.6 8.9 %multiply_add_fusion = f32[512,512]{1,0:T(8,128)S(1)} fusion(f32[512,128]{1,0:T(8,128)S(1)} %all-gather, f32[512,128]{1,0:T(8,128)S(1)} %copy-done.3, f32[512]{0:T(512)S(1)} %multiply_add_fusion.1, f32[512]{0:T(512)S(1)} %multiply_add_fusion.2), kind=kOutput, calls=%fused_computation.11 | convolution fusion | flops 414187520 | bytes 1576960 | tf_op jit(solution)/shard_map/dot_general | solution.py:14
  77.6 1.8 fusion.8
  79.4 0.2 copy.24
  79.6 0.6 gather_fusion.1
  80.2 30.8 %all-gather.1 = f32[512,64]{1,0:T(8,128)S(1)} all-gather(f32[64,64]{1,0:T(8,128)S(1)} %gather_fusion.1), channel_id=3, replica_groups=mesh['batch'=4,'centers'=8] {'centers'}, dimensions={0}, use_global_device_ids=true | all-gather | bytes 147456 | tf_op jit(solution)/shard_map/all_gather | solution.py:63
  111.1 0.1 copy.25
  111.2 0.1 reshape.100
  111.3 39.5 %all-reduce.4.cloned.1.call-done = f32[512,64]{0,1:T(8,128)} async-done(((f32[512,64]{0,1:T(8,128)}), f32[512,64]{0,1:T(8,128)}) %all-reduce.4.cloned.1.call-update) | async-done | bytes 131088 | tf_op jit(solution)/shard_map/psum | solution.py:64
  150.8 0.9 sub.36
  151.7 1.4 convolution_multiply_fusion.1
  153.3 31.3 %all-reduce.6.cloned.1.call-done = f32[512,64]{0,1:T(8,128)} async-done(((f32[512,64]{0,1:T(8,128)}), f32[512,64]{0,1:T(8,128)}) %all-reduce.6.cloned.1.call-update) | async-done | bytes 131088 | tf_op jit(solution)/shard_map/psum | solution.py:76
  184.6 1.0 copy.27
  185.6 0.7 gather_fusion.2
  186.3 0.1 reshape.114
  186.5 12.2 %all_to_all.22 = f32[8,1,2048]{2,1,0:T(1,128)S(1)} all-to-all(f32[8,1,2048]{2,1,0:T(1,128)S(1)} %reshape.114), channel_id=1, replica_groups=mesh['batch'=4,'centers'=8] {'centers'}, dimensions={0} | all-to-all | bytes 131072 | tf_op jit(solution)/shard_map/all_to_all | solution.py:86
  198.7 0.5 broadcast.212
  199.2 0.8 reduce
  200.0 0.1 reshape.115
  200.1 1.2 gather_fusion.3
  201.3 1.1 convolution_bitcast_fusion
  202.5 123.4 %all-reduce.8.cloned.1.call-done = f32[1024,64]{0,1:T(8,128)} async-done(((f32[1024,64]{0,1:T(8,128)}), f32[1024,64]{0,1:T(8,128)}) %all-reduce.8.cloned.1.call-update) | async-done | bytes 262160 | tf_op jit(solution)/shard_map/psum | solution.py:95
  325.9 1.6 convolution_bitcast_fusion.1
  327.5 0.1 copy.28
  327.6 6.9 %scatter_fusion.1 = f32[8,32,64]{2,1,0:T(8,128)S(1)} fusion(f32[8,32,64]{2,1,0:T(8,128)S(1)} %broadcast_in_dim.8, s32[128]{0:T(128)S(1)} %get-tuple-element.8, f32[128,64]{1,0:T(8,128)S(1)} %copy.28), kind=kCustom, calls=%fused_computation.5 | custom fusion | bytes 99328 | tf_op jit(solution)/shard_map/scatter | solution.py:103
  334.6 0.1 reshape.116
  334.7 11.2 %all_to_all.23 = f32[8,1,2048]{2,1,0:T(1,128)S(1)} all-to-all(f32[8,1,2048]{2,1,0:T(1,128)S(1)} %reshape.116), channel_id=1, replica_groups=mesh['batch'=4,'centers'=8] {'centers'}, dimensions={0} | all-to-all | bytes 131072 | tf_op jit(solution)/shard_map/all_to_all | solution.py:105
  345.9 0.8 reduce.1
  346.7 0.1 reshape.117
  346.8 1.7 scatter_custom_fusion.2
  348.5 0.1 copy.30
  348.7 0.1 collective-permute-start
  348.7 1.3 collective-permute-done
  350.1 0.7 collective-permute-start.1
  350.8 0.1 constant_dynamic-slice_fusion
  350.9 0.7 copy.31
  351.6 4.1 %collective-permute-done.1 = f32[512,64]{0,1:T(8,128)S(1)} collective-permute-done((f32[512,64]{0,1:T(8,128)S(1)}, f32[512,64]{0,1:T(8,128)S(1)}, u32[]{:S(2)}, u32[]{:S(2)}) %collective-permute-start.1) | collective-permute-done | bytes 131104 | tf_op jit(solution)/shard_map/ppermute | solution.py:110
  355.7 0.7 add_subtract_fusion
  (35 shorter events, 0.3 us)
Async XLA Ops:
  7.2 194.2 %copy-start = (f32[128,1024]{1,0:T(8,128)S(1)}, f32[128,1024]{1,0:T(8,128)}, u32[]{:S(2)}) copy-start(f32[128,1024]{1,0:T(8,128)} %param.14) | copy-start | bytes 1572868
  7.2 0.7 copy-start.6
  8.3 0.7 copy-start.8
  9.0 27.4 %copy-start.3 = (f32[512,128]{1,0:T(8,128)S(1)}, f32[512,128]{1,0:T(8,128)}, u32[]{:S(2)}) copy-start(f32[512,128]{1,0:T(8,128)} %param.12) | copy-start | bytes 786436
  9.0 27.6 %copy-start.5 = (f32[1024,128]{1,0:T(8,128)S(1)}, f32[1024,128]{1,0:T(8,128)}, u32[]{:S(2)}) copy-start(f32[1024,128]{1,0:T(8,128)} %param.9) | copy-start | bytes 1572868
  28.9 7.5 %copy-start.9 = (s32[64]{0:T(128)S(1)}, s32[64]{0:T(128)}, u32[]{:S(2)}) copy-start(s32[64]{0:T(128)} %param.11) | copy-start | bytes 772
  28.9 82.3 %all-to-all-start = ((s32[8,1,32]{2,1,0:T(1,128)}), s32[8,1,32]{2,1,0:T(1,128)S(1)}, u32[]{:S(2)}, u32[]{:S(2)}) async-start(s32[8,1,32]{2,1,0:T(1,128)} %bitcast.4), calls=%async_computation | async-start | bytes 8192 | tf_op jit(solution)/shard_map/all_to_all | solution.py:84
  36.3 114.5 %all-reduce.4.cloned.1.call-start = ((), (), s32[]{:S(2)}) async-start(), calls=%async_computation.3 | async-start | bytes 262144 | tf_op jit(solution)/shard_map/psum | solution.py:64
  68.6 8.9 %copy-start.4 = (f32[512,64]{0,1:T(8,128)S(1)}, f32[512,64]{0,1:T(8,128)}, u32[]{:S(2)}) copy-start(f32[512,64]{0,1:T(8,128)} %param.13) | copy-start | bytes 393220
  77.5 1.9 copy-start.2
  79.4 105.2 %all-reduce.6.cloned.1.call-start = ((), (), s32[]{:S(2)}) async-start(), calls=%async_computation.4 | async-start | bytes 262144 | tf_op jit(solution)/shard_map/psum | solution.py:76
  153.2 172.7 %all-reduce.8.cloned.1.call-start = ((), (), s32[]{:S(2)}) async-start(), calls=%async_computation.5 | async-start | bytes 524288 | tf_op jit(solution)/shard_map/psum | solution.py:95
  202.5 123.4 %copy-start.7 = (f32[1024]{0:T(1024)S(1)}, f32[1024]{0:T(1024)}, u32[]{:S(2)}) copy-start(f32[1024]{0:T(1024)} %param.15) | copy-start | bytes 12292
  348.7 1.4 collective-permute-start
  350.1 5.6 %copy-start.1 = (f32[512,64]{0,1:T(8,128)S(1)}, f32[512,64]{0,1:T(8,128)}, u32[]{:S(2)}) copy-start(f32[512,64]{0,1:T(8,128)} %all-reduce.6.cloned.1.call-done) | copy-start | bytes 393220
  350.1 5.6 %collective-permute-start.1 = (f32[512,64]{0,1:T(8,128)S(1)}, f32[512,64]{0,1:T(8,128)S(1)}, u32[]{:S(2)}, u32[]{:S(2)}) collective-permute-start(f32[512,64]{0,1:T(8,128)S(1)} %add.95), channel_id=1, source_target_pairs={{0,16},{8,24},{16,0},{24,8},{1,17},{9,25},{17,1},{25,9},{2,18},{10... | collective-permute-start | bytes 393224 | tf_op jit(solution)/shard_map/ppermute | solution.py:110
Sparse Core Ops, SparseCore 0:
  79.5 71.2 all-reduce.3
  153.7 30.8 all-reduce.5
  202.6 123.2 all-reduce.7
